TPU v7x, 32 devices: a whole 2x2x4 slice. The times are simulated.
32 devices in a mesh: groups: 2 (over y), inner: 4 (over z), outer: 4 (over x, core).
Axes of the slice: x: 2, y: 2, z: 4, core: 2. Of those that a mesh axis runs over, the one named last changes fastest.
Arguments:
- queries: bfloat16 [8192, 1024], P(('groups', 'outer', 'inner')), parts along dimension 0, may hold values from -6 to 6
- keys: bfloat16 [8192, 1024], P(('groups', 'outer', 'inner')), parts along dimension 0, may hold values from -6 to 6
- values: bfloat16 [8192, 1024], P(('groups', 'outer', 'inner')), parts along dimension 0, may hold values from -6 to 6
- retain: float32 [8192, 8], P(('groups', 'outer', 'inner')), parts along dimension 0, may hold values from 0.4 to 1
- step: float32 [8192, 8], P(('groups', 'outer', 'inner')), parts along dimension 0, may hold values from 0.000625 to 0.0125
- momentum: float32 [8192, 8], P(('groups', 'outer', 'inner')), parts along dimension 0, may hold values from 0.97 to 0.99
- init_memory: float32 [8, 128, 128], replicated, may hold values from -0.1875 to 0.1875
- init_momentum: float32 [8, 128, 128], replicated, may hold values from -0.1875 to 0.1875
Outputs:
- retrieved: bfloat16 [8192, 1024], P(('groups', 'outer', 'inner')), parts along dimension 0
There are 2 independent parts, one for each index of `groups`. A program takes and returns all parts, laid end to end along the dimension named above; an argument that names none is the same for every part. Nothing has to cross between parts.
All inputs are finite; a program needn't handle non-finite values.
Results may differ from a plain program's by a relative error of at most 0.001.
Values sent between devices are 32-bit elements; how exact they have to be, the bound alone decides.
No kernel may reach another device: no remote copies, remote signals or barrier semaphores. Data moves between devices by JAX's collectives and lax.ppermute only.
A program may use at most 256 MiB of HBM per device.

v0:
```python
import jax
import jax.numpy as jnp
from jax import lax
from jax.sharding import PartitionSpec as P


def carried_in(value, axis, join, neutral):
    count, mine = (lax.axis_size(axis), lax.axis_index(axis))
    pieces = jax.tree.map(lambda part: lax.all_gather(part, axis), value)
    total = jax.tree.map(
        lambda part, zero: jnp.full_like(part, 0) + jnp.asarray(zero, part.dtype), value, neutral
    )

    def turn(position, total):
        longer = join(total, jax.tree.map(lambda part: part[position], pieces))
        return jax.tree.map(lambda new, old: jnp.where(position < mine, new, old), longer, total)

    return lax.fori_loop(0, count - 1, turn, total)


def from_root(block, axis, owner):
    block = jnp.where(lax.axis_index(axis) == owner, block, jnp.zeros_like(block))
    return lax.psum(block, axis)


def unit_rows(source, heads):
    rows = source.astype(jnp.float32).reshape(source.shape[0], heads, -1)
    return rows * lax.rsqrt(jnp.sum(rows * rows, -1, keepdims=True) + 1e-06)


def block_terms(queries, keys, values, retain, step, momentum):
    length = queries.shape[0]
    heads = retain.shape[1]
    precise = lax.Precision.HIGHEST
    query_unit = unit_rows(queries, heads)
    key_unit = unit_rows(keys, heads)
    value_rows = values.astype(jnp.float32).reshape(length, heads, -1)
    key_width = key_unit.shape[2]
    log_retain = jnp.cumsum(jnp.log(retain), 0).T
    log_moment = jnp.cumsum(jnp.log(momentum), 0).T
    position = jnp.arange(length)
    causal = (position[:, None] >= position[None, :])[None]
    retain_decay = jnp.where(
        causal,
        jnp.exp(jnp.where(causal, log_retain[:, :, None] - log_retain[:, None, :], 0.0)),
        0.0,
    )
    momentum_decay = jnp.where(
        causal,
        jnp.exp(jnp.where(causal, log_moment[:, :, None] - log_moment[:, None, :], 0.0)),
        0.0,
    )
    weights = jnp.einsum("htu,hur->htr", retain_decay, momentum_decay, precision=precise)
    carry_scale = jnp.einsum("htu,hu->ht", retain_decay, jnp.exp(log_moment), precision=precise)
    scores = jnp.einsum("thd,rhd->htr", query_unit, key_unit, precision=precise)
    step_rows = step.T
    mixing = scores * weights * step_rows[:, None, :]
    memory_weight = weights[:, -1, :] * step_rows
    moment_weight = jnp.exp(log_moment[:, -1:] - log_moment) * step_rows
    memory_gram = jnp.einsum(
        "rhd,hr,rhe->hde", key_unit, memory_weight, key_unit, precision=precise
    )
    moment_gram = jnp.einsum(
        "rhd,hr,rhe->hde", key_unit, moment_weight, key_unit, precision=precise
    )
    identity = jnp.eye(key_width, dtype=jnp.float32)[None]
    retain_end = jnp.exp(log_retain[:, -1])[:, None, None]
    moment_end = jnp.exp(log_moment[:, -1])[:, None, None]
    carry_end = carry_scale[:, -1][:, None, None]
    upper_rows = jnp.concatenate([retain_end * identity - memory_gram, -moment_gram], axis=2)
    lower_rows = jnp.concatenate([carry_end * identity, moment_end * identity], axis=2)
    transition = jnp.concatenate([upper_rows, lower_rows], axis=1)
    memory_write = jnp.einsum(
        "rhd,hr,rhe->hde", value_rows, memory_weight, key_unit, precision=precise
    )
    moment_write = jnp.einsum(
        "rhd,hr,rhe->hde", value_rows, moment_weight, key_unit, precision=precise
    )
    offset = jnp.concatenate([memory_write, moment_write], axis=2)
    local_terms = (query_unit, key_unit, value_rows, jnp.exp(log_retain), carry_scale, mixing)
    return (transition, offset, local_terms)


def block_output(carried, local_terms):
    query_unit, key_unit, value_rows, retain_scale, carry_scale, mixing = local_terms
    precise = lax.Precision.HIGHEST
    key_width = query_unit.shape[2]
    memory = carried[:, :, :key_width]
    moment_part = carried[:, :, key_width:]
    residual = jnp.einsum("rhd,hed->hre", key_unit, memory, precision=precise) - jnp.transpose(
        value_rows, (1, 0, 2)
    )
    result = retain_scale[:, :, None] * jnp.einsum(
        "thd,hed->hte", query_unit, memory, precision=precise
    )
    result = result + carry_scale[:, :, None] * jnp.einsum(
        "thd,hed->hte", query_unit, moment_part, precision=precise
    )
    result = result - jnp.einsum("htr,hre->hte", mixing, residual, precision=precise)
    return jnp.transpose(result, (1, 0, 2)).reshape(query_unit.shape[0], -1).astype(jnp.bfloat16)


def advance_state(carried, transition, offset):
    return jnp.einsum("hij,hjk->hik", carried, transition, precision=lax.Precision.HIGHEST) + offset


def compose(earlier, later):
    joined = jnp.einsum("hij,hjk->hik", earlier[0], later[0], precision=lax.Precision.HIGHEST)
    return (joined, advance_state(earlier[1], later[0], later[1]))


def apply_earlier(gathered, first_state):
    my_group = lax.axis_index("outer")

    def advance_group(index, carried):
        moved = advance_state(carried, gathered[0][index], gathered[1][index])
        return jnp.where(index < my_group, moved, carried)

    return lax.fori_loop(0, gathered[0].shape[0], advance_group, first_state)


def local(queries, keys, values, retain, step, momentum, init_memory, init_momentum):
    transition, offset, local_terms = block_terms(queries, keys, values, retain, step, momentum)
    identity_maps = (
        jnp.broadcast_to(jnp.eye(transition.shape[1], dtype=jnp.float32), transition.shape),
        jnp.zeros_like(offset),
    )
    before = carried_in((transition, offset), "inner", compose, identity_maps)
    through = compose(before, (transition, offset))
    first_state = jnp.concatenate([init_memory, init_momentum], axis=2)
    last_inner = lax.axis_size("inner") - 1
    group_map = (
        from_root(through[0], "inner", last_inner),
        from_root(through[1], "inner", last_inner),
    )
    gathered = (
        lax.all_gather(group_map[0][None], "outer", axis=0, tiled=True),
        lax.all_gather(group_map[1][None], "outer", axis=0, tiled=True),
    )
    entry_state = apply_earlier(gathered, first_state)
    block_state = advance_state(entry_state, before[0], before[1])
    return block_output(block_state, local_terms)


def solution(mesh):
    placed = (
        P(("groups", "outer", "inner"), None),
        P(("groups", "outer", "inner"), None),
        P(("groups", "outer", "inner"), None),
        P(("groups", "outer", "inner"), None),
        P(("groups", "outer", "inner"), None),
        P(("groups", "outer", "inner"), None),
        P(),
        P(),
    )
    return jax.shard_map(
        local,
        mesh=mesh,
        in_specs=placed,
        out_specs=P(("groups", "outer", "inner"), None),
        check_vma=False,
    )
```

profile of v0, /device:TPU:0, one launch (start us, length us, event | category | flops | bytes accessed | tf_op | source)
XLA Modules:
  0.0 601.0 jit_solution(4477719836671399538)
XLA Ops:
  10.5 2.9 fusion.39
  18.3 2.1 broadcast_multiply_fusion.1
  22.7 2.0 copy.120
  29.2 2.6 copy.125
  32.2 2.3 fusion.44
  38.9 1.8 copy.119
  41.4 74.1 %all-gather.13.cloned.1.call-done = f32[32,128,256]{2,1,0:T(8,128)} async-done(((f32[8,128,256]{2,1,0:T(8,128)}), f32[32,128,256]{2,1,0:T(8,128)}) %all-gather.13.cloned.1.call-update) | async-done | bytes 4194320 | tf_op jit(solution)/shard_map/all_gather | solution.py:9
  115.4 149.8 %all-gather.11.cloned.1.call-done = f32[32,256,256]{2,1,0:T(8,128)} async-done(((f32[8,256,256]{2,1,0:T(8,128)}), f32[32,256,256]{2,1,0:T(8,128)}) %all-gather.11.cloned.1.call-update) | async-done | bytes 8388624 | tf_op jit(solution)/shard_map/all_gather | solution.py:9
  265.4 49.7 %while.30 = (s32[]{:T(128)}, f32[8,256,256]{1,2,0:T(8,128)S(1)}, f32[8,128,256]{1,2,0:T(8,128)}, s32[]{:T(128)}, f32[4,8,256,256]{3,2,1,0:T(8,128)}, /*index=5*/f32[4,8,128,256]{3,2,1,0:T(8,128)}, s32[]{:T(128)}, s32[]{:T(128)}) while((s32[]{:T(128)}, f32[8,256,256]{1,2,0:T(8,128)S(1)}, f32[8,128,256]{1,2,0:T(8,128)}, s32[]{:T(128)}, ...), condition=%wide.region_7.8_spmd.clone, body=%wide.region_6.7_spmd.clone.sunk | while | flops 2417491968 | bytes 25168492 | solution.py:18
  265.4 2.3 constant_dynamic-slice_fusion.5
  270.5 6.1 %fusion.112 = f32[8,128,256]{1,2,0:T(8,128)} fusion(f32[4,8,256,256]{3,2,1,0:T(8,128)} %get-tuple-element.387, s32[]{:T(128)} %get-tuple-element.375, f32[1,8,128,256]{2,3,1,0:T(8,128)S(1)} %copy.193, f32[8,128,256]{1,2,0:T(8,128)S(1)} %copy.218, pred[]{:T(512)S(6)} %compare.3, pred[]{:T(512)S(6)} %lt.44), kind=kOutput, calls=%fused_computation.17.clone.1 | convolution fusion | flops 806354944 | bytes 6293504 | tf_op jit(solution)/shard_map/while/body/eval_jaxpr/hij,hjk->hik/dot_general | solution.py:104
  276.8 5.1 bitcast_select_fusion.2
  281.9 2.3 constant_dynamic-slice_fusion.5
  287.0 6.1 %fusion.112 = f32[8,128,256]{1,2,0:T(8,128)} fusion(f32[4,8,256,256]{3,2,1,0:T(8,128)} %get-tuple-element.387, s32[]{:T(128)} %get-tuple-element.375, f32[1,8,128,256]{2,3,1,0:T(8,128)S(1)} %copy.193, f32[8,128,256]{1,2,0:T(8,128)S(1)} %copy.218, pred[]{:T(512)S(6)} %compare.3, pred[]{:T(512)S(6)} %lt.44), kind=kOutput, calls=%fused_computation.17.clone.1 | convolution fusion | flops 806354944 | bytes 6293504 | tf_op jit(solution)/shard_map/while/body/eval_jaxpr/hij,hjk->hik/dot_general | solution.py:104
  293.3 5.1 bitcast_select_fusion.2
  298.4 2.3 constant_dynamic-slice_fusion.5
  303.5 6.1 %fusion.112 = f32[8,128,256]{1,2,0:T(8,128)} fusion(f32[4,8,256,256]{3,2,1,0:T(8,128)} %get-tuple-element.387, s32[]{:T(128)} %get-tuple-element.375, f32[1,8,128,256]{2,3,1,0:T(8,128)S(1)} %copy.193, f32[8,128,256]{1,2,0:T(8,128)S(1)} %copy.218, pred[]{:T(512)S(6)} %compare.3, pred[]{:T(512)S(6)} %lt.44), kind=kOutput, calls=%fused_computation.17.clone.1 | convolution fusion | flops 806354944 | bytes 6293504 | tf_op jit(solution)/shard_map/while/body/eval_jaxpr/hij,hjk->hik/dot_general | solution.py:104
  309.8 5.1 bitcast_select_fusion.2
  315.1 5.2 fusion.49
  320.3 4.8 select_bitcast_fusion
  325.2 119.8 %all-reduce.3.cloned.1.call-done = (f32[1,8,256,256]{3,2,1,0:T(8,128)}, f32[1,8,128,256]{2,3,1,0:T(8,128)}) async-done(((f32[1,8,256,256]{3,2,1,0:T(8,128)}, f32[1,8,128,256]{2,3,1,0:T(8,128)}), (f32[1,8,256,256]{3,2,1,0:T(8,128)}, f32[1,8,128,256]{2,3,1,0:T(8,128)})) %all-reduce.3.cloned.1.call-update) | async-done | bytes 3145744 | tf_op jit(solution)/shard_map/psum | solution.py:23
  445.0 2.5 copy.133
  452.1 5.1 fusion.66
  458.5 22.6 %all-gather.9.cloned.1.call-done = f32[4,8,128,256]{3,2,1,0:T(8,128)} async-done(((f32[1,8,128,256]{3,2,1,0:T(8,128)}), f32[4,8,128,256]{3,2,1,0:T(8,128)}) %all-gather.9.cloned.1.call-update) | async-done | bytes 4194320 | tf_op jit(solution)/shard_map/all_gather | solution.py:138
  481.2 59.7 %all-gather.7.cloned.1.call-done = f32[4,8,256,256]{3,2,1,0:T(8,128)} async-done(((f32[1,8,256,256]{3,2,1,0:T(8,128)}), f32[4,8,256,256]{3,2,1,0:T(8,128)}) %all-gather.7.cloned.1.call-update) | async-done | bytes 8388624 | tf_op jit(solution)/shard_map/all_gather | solution.py:137
  540.9 41.4 %while.29 = (s32[]{:T(128)}, f32[8,128,256]{1,2,0:T(8,128)}, s32[]{:T(128)}, f32[4,8,256,256]{3,2,1,0:T(8,128)}, f32[4,8,128,256]{3,2,1,0:T(8,128)}, /*index=5*/s32[]{:T(128)}) while((s32[]{:T(128)}, f32[8,128,256]{1,2,0:T(8,128)}, s32[]{:T(128)}, f32[4,8,256,256]{3,2,1,0:T(8,128)}, f32[4,8,128,256]{3,2,1,0:T(8,128)}, ...), condition=%wide.region_11.12_spmd, body=%wide.region_10.11_spmd.sunk | while | flops 805830656 | bytes 16777840 | solution.py:119
  545.3 6.1 %fusion.107 = f32[8,128,256]{1,2,0:T(8,128)} fusion(f32[8,128,256]{1,2,0:T(8,128)S(1)} %copy.216, f32[4,8,256,256]{3,2,1,0:T(8,128)} %get-tuple-element.406, s32[]{:T(128)} %get-tuple-element.397, f32[1,8,128,256]{2,3,1,0:T(8,128)S(1)} %copy-done, pred[]{:T(512)S(6)} %lt.43), kind=kOutput, calls=%fused_computation.5.clone.1 | convolution fusion | flops 805830656 | bytes 6291969 | tf_op jit(solution)/shard_map/while/body/eval_jaxpr/hij,hjk->hik/dot_general | solution.py:104
  555.6 6.1 %fusion.107 = f32[8,128,256]{1,2,0:T(8,128)} fusion(f32[8,128,256]{1,2,0:T(8,128)S(1)} %copy.216, f32[4,8,256,256]{3,2,1,0:T(8,128)} %get-tuple-element.406, s32[]{:T(128)} %get-tuple-element.397, f32[1,8,128,256]{2,3,1,0:T(8,128)S(1)} %copy-done, pred[]{:T(512)S(6)} %lt.43), kind=kOutput, calls=%fused_computation.5.clone.1 | convolution fusion | flops 805830656 | bytes 6291969 | tf_op jit(solution)/shard_map/while/body/eval_jaxpr/hij,hjk->hik/dot_general | solution.py:104
  565.9 6.1 %fusion.107 = f32[8,128,256]{1,2,0:T(8,128)} fusion(f32[8,128,256]{1,2,0:T(8,128)S(1)} %copy.216, f32[4,8,256,256]{3,2,1,0:T(8,128)} %get-tuple-element.406, s32[]{:T(128)} %get-tuple-element.397, f32[1,8,128,256]{2,3,1,0:T(8,128)S(1)} %copy-done, pred[]{:T(512)S(6)} %lt.43), kind=kOutput, calls=%fused_computation.5.clone.1 | convolution fusion | flops 805830656 | bytes 6291969 | tf_op jit(solution)/shard_map/while/body/eval_jaxpr/hij,hjk->hik/dot_general | solution.py:104
  576.2 6.1 %fusion.107 = f32[8,128,256]{1,2,0:T(8,128)} fusion(f32[8,128,256]{1,2,0:T(8,128)S(1)} %copy.216, f32[4,8,256,256]{3,2,1,0:T(8,128)} %get-tuple-element.406, s32[]{:T(128)} %get-tuple-element.397, f32[1,8,128,256]{2,3,1,0:T(8,128)S(1)} %copy-done, pred[]{:T(512)S(6)} %lt.43), kind=kOutput, calls=%fused_computation.5.clone.1 | convolution fusion | flops 805830656 | bytes 6291969 | tf_op jit(solution)/shard_map/while/body/eval_jaxpr/hij,hjk->hik/dot_general | solution.py:104
  582.3 4.0 convolution_add_fusion
  589.4 2.5 fusion.45
  (157 shorter events, 57.5 us)
Async XLA Ops:
  6.5 108.9 %all-gather.13.cloned.1.call-start = ((), (), s32[]{:S(2)}) async-start(), calls=%async_computation.3 | async-start | bytes 5242880 | tf_op jit(solution)/shard_map/all_gather | solution.py:9
  6.6 6.9 %copy-start.25 = (pred[256,256]{1,0:T(8,128)(4,1)}, pred[256,256]{1,0:T(8,128)(4,1)S(1)}, u32[]{:S(2)}) copy-start(pred[256,256]{1,0:T(8,128)(4,1)S(1)} %iota_compare_fusion) | copy-start | bytes 196612
  8.2 5.3 copy-start.28
  10.5 3.0 copy-start.31
  10.5 3.0 copy-start.27
  10.5 4.4 copy-start.21
  18.3 2.1 copy-start.23
  20.4 16.1 %copy-start.2 = (f32[256,8,128]{2,1,0:T(8,128)}, f32[256,8,128]{2,1,0:T(8,128)S(1)}, u32[]{:S(2)}) copy-start(f32[256,8,128]{2,1,0:T(8,128)S(1)} %get-tuple-element.291) | copy-start | bytes 3145732
  24.8 1.7 copy-start.6
  29.2 3.0 copy-start.32
  29.2 3.0 copy-start.26
  29.2 3.0 copy-start.29
  29.2 3.0 copy-start.30
  31.8 233.4 %all-gather.11.cloned.1.call-start = ((), (), s32[]{:S(2)}) async-start(), calls=%async_computation.2 | async-start | bytes 10485760 | tf_op jit(solution)/shard_map/all_gather | solution.py:9
  35.1 2.9 copy-start.8
  35.1 2.9 copy-start.10
  40.7 404.2 %all-reduce.3.cloned.1.call-start = ((), (), s32[]{:S(2)}) async-start(), calls=%async_computation.4 | async-start | bytes 6291456 | tf_op jit(solution)/shard_map/psum | solution.py:23
  315.1 5.2 copy-start.9
  315.1 5.2 copy-start.11
  315.1 5.2 copy-start.13
  315.1 5.2 copy-start.15
  325.2 156.0 %all-gather.9.cloned.1.call-start = ((), (), s32[]{:S(2)}) async-start(), calls=%async_computation.1 | async-start | bytes 5242880 | tf_op jit(solution)/shard_map/all_gather | solution.py:138
  447.5 2.0 copy-start.24
  447.5 93.4 %all-gather.7.cloned.1.call-start = ((), (), s32[]{:S(2)}) async-start(), calls=%async_computation | async-start | bytes 10485760 | tf_op jit(solution)/shard_map/all_gather | solution.py:137
  452.1 5.1 copy-start.1
  543.8 1.5 copy-start
  554.1 1.5 copy-start
  564.4 1.5 copy-start
  574.7 1.5 copy-start
  582.3 4.0 copy-start.4
  586.3 2.5 copy-start.17
  587.6 1.7 copy-start.5
  (9 other events, 9.9 us)
Sparse Core Ops, SparseCore 0:
  31.9 83.4 all-gather.12
  117.0 148.1 all-gather.10
  325.3 119.6 all-reduce.2
  447.7 33.4 all-gather.8
  482.6 58.2 all-gather.6
where the time goes:
time: 609 us; the launch traced here: 601 us
  waiting for transfers between devices  427 us (70%)
  matrix products  93.8 us (15%)
  local copies, waits for them, and re-layouts  56.5 us (9%)
  between operations  13.9 us (2%)
  other arithmetic  8.6 us (1%)
    all_gather x2, waiting for transfers between devices, carried_in(): pieces = jax.tree.map(lambda part: lax.all_gather(part, axis), value)  224 us
    psum x1, waiting for transfers between devices, from_root(): return lax.psum(block, axis)  120 us
    all_gather x1, waiting for transfers between devices, local(): lax.all_gather(group_map[0][None], 'outer', axis=0, tiled=True)  59.7 us
    dot_general x9, matrix products, advance_state(): jnp.einsum('hij,hjk->hik', carried, transition, precision=lax.Precision.H...  51.8 us
    all_gather x1, waiting for transfers between devices, local(): lax.all_gather(group_map[1][None], 'outer', axis=0, tiled=True)  22.6 us
    dot_general x4, matrix products, compose(): jnp.einsum('hij,hjk->hik', earlier[0], later[0], precision=lax.Precision....  20.2 us
  transfers between devices with their start and end apart: 5, of which 5 were waited for; matrix products, arithmetic and copies ran while one was open for 3% of the time, Pallas kernels for 0%

commit v1 on v0

--- a/solution.py
+++ b/solution.py
@@ -20,7 +20,7 @@
 
 def from_root(block, axis, owner):
     block = jnp.where(lax.axis_index(axis) == owner, block, jnp.zeros_like(block))
-    return lax.psum(block, axis)
+    return jnp.sum(lax.all_gather(block, axis), axis=0)
 
 
 def unit_rows(source, heads):

time: 609 us -> 713 us (1.17)
  waiting for transfers between devices: 427 us -> 520 us
  other arithmetic: 8.6 us -> 17.1 us
    all_gather x0 -> x2, waiting for transfers between devices: none -> 219 us  [from_root(): return jnp.sum(lax.all_gather(block, axis), axis=0)]
    psum x1 -> x0, waiting for transfers between devices: 120 us -> none  [from_root(): return lax.psum(block, axis)]
    reduce_sum x0 -> x2, other arithmetic: none -> 9.17 us  [from_root(): return jnp.sum(lax.all_gather(block, axis), axis=0)]
  transfers between devices with their start and end apart: 5 -> 6, of which waited for: 5 -> 6; matrix products, arithmetic and copies ran while one was open for 3% -> 5% of each run, Pallas kernels for 0% -> 0%
where the time goes in v1:
time: 713 us; the launch traced here: 705 us
  waiting for transfers between devices  520 us (73%)
  matrix products  94.7 us (13%)
  local copies, waits for them, and re-layouts  57.5 us (8%)
  other arithmetic  17.1 us (2%)
  between operations  14.3 us (2%)
    all_gather x2, waiting for transfers between devices, carried_in(): pieces = jax.tree.map(lambda part: lax.all_gather(part, axis), value)  224 us
    all_gather x2, waiting for transfers between devices, from_root(): return jnp.sum(lax.all_gather(block, axis), axis=0)  219 us
    all_gather x1, waiting for transfers between devices, local(): lax.all_gather(group_map[0][None], 'outer', axis=0, tiled=True)  59.7 us
    dot_general x9, matrix products, advance_state(): jnp.einsum('hij,hjk->hik', carried, transition, precision=lax.Precision.H...  51.6 us
    dot_general x4, matrix products, compose(): jnp.einsum('hij,hjk->hik', earlier[0], later[0], precision=lax.Precision....  21.4 us
    all_gather x1, waiting for transfers between devices, local(): lax.all_gather(group_map[1][None], 'outer', axis=0, tiled=True)  17.6 us
  transfers between devices with their start and end apart: 6, of which 6 were waited for; matrix products, arithmetic and copies ran while one was open for 5% of the time, Pallas kernels for 0%

profile of v1, /device:TPU:0, one launch (start us, length us, event | category | flops | bytes accessed | tf_op | source)
XLA Modules:
  0.0 705.1 jit_solution(14355368479321419354)
XLA Ops:
  10.5 2.9 fusion.39
  28.6 2.6 copy.121
  31.6 2.3 fusion.44
  40.8 74.1 %all-gather.15.cloned.1.call-done = f32[32,128,256]{2,1,0:T(8,128)} async-done(((f32[8,128,256]{2,1,0:T(8,128)}), f32[32,128,256]{2,1,0:T(8,128)}) %all-gather.15.cloned.1.call-update) | async-done | bytes 4194320 | tf_op jit(solution)/shard_map/all_gather | solution.py:9
  114.9 149.8 %all-gather.13.cloned.1.call-done = f32[32,256,256]{2,1,0:T(8,128)} async-done(((f32[8,256,256]{2,1,0:T(8,128)}), f32[32,256,256]{2,1,0:T(8,128)}) %all-gather.13.cloned.1.call-update) | async-done | bytes 8388624 | tf_op jit(solution)/shard_map/all_gather | solution.py:9
  264.8 49.5 %while.30 = (s32[]{:T(128)}, f32[8,256,256]{1,2,0:T(8,128)S(1)}, f32[8,128,256]{1,2,0:T(8,128)}, s32[]{:T(128)}, f32[4,8,256,256]{3,2,1,0:T(8,128)}, /*index=5*/f32[4,8,128,256]{3,2,1,0:T(8,128)}, s32[]{:T(128)}, s32[]{:T(128)}) while((s32[]{:T(128)}, f32[8,256,256]{1,2,0:T(8,128)S(1)}, f32[8,128,256]{1,2,0:T(8,128)}, s32[]{:T(128)}, ...), condition=%wide.region_7.8_spmd.clone, body=%wide.region_6.7_spmd.clone.sunk | while | flops 2417491968 | bytes 25168492 | solution.py:18
  264.8 2.3 constant_dynamic-slice_fusion.5
  269.9 6.1 fusion.111
  276.2 5.1 bitcast_select_fusion.2
  281.3 2.3 constant_dynamic-slice_fusion.5
  286.4 6.1 fusion.111
  292.7 5.1 bitcast_select_fusion.2
  297.8 2.3 constant_dynamic-slice_fusion.5
  302.9 6.1 fusion.111
  309.1 5.1 bitcast_select_fusion.2
  314.3 5.0 fusion.48
  319.3 2.6 copy.129
  322.2 6.0 convolution_select_fusion
  328.3 72.8 %all-gather.21.cloned.1.call-done = f32[32,128,256]{2,1,0:T(8,128)} async-done(((f32[8,128,256]{2,1,0:T(8,128)}), f32[32,128,256]{2,1,0:T(8,128)}) %all-gather.21.cloned.1.call-update) | async-done | bytes 4194320 | tf_op jit(solution)/shard_map/all_gather | solution.py:23
  401.1 3.6 reduce_sum.39
  404.8 145.9 %all-gather.17.cloned.1.call-done = f32[32,256,256]{2,1,0:T(8,128)} async-done(((f32[8,256,256]{2,1,0:T(8,128)}), f32[32,256,256]{2,1,0:T(8,128)}) %all-gather.17.cloned.1.call-update) | async-done | bytes 8388624 | tf_op jit(solution)/shard_map/all_gather | solution.py:23
  550.8 5.6 reduce_sum.38
  561.1 4.9 fusion.65
  567.3 17.6 %all-gather.23.cloned.1.call-done = f32[32,128,256]{2,1,0:T(8,128)} async-done(((f32[8,128,256]{2,1,0:T(8,128)}), f32[32,128,256]{2,1,0:T(8,128)}) %all-gather.23.cloned.1.call-update) | async-done | bytes 4194320 | tf_op jit(solution)/shard_map/all_gather | solution.py:138
  584.9 59.7 %all-gather.19.cloned.1.call-done = f32[32,256,256]{2,1,0:T(8,128)} async-done(((f32[8,256,256]{2,1,0:T(8,128)}), f32[32,256,256]{2,1,0:T(8,128)}) %all-gather.19.cloned.1.call-update) | async-done | bytes 8388624 | tf_op jit(solution)/shard_map/all_gather | solution.py:137
  644.6 41.4 %while.29 = (s32[]{:T(128)}, f32[8,128,256]{1,2,0:T(8,128)}, s32[]{:T(128)}, f32[4,8,256,256]{3,2,1,0:T(8,128)}, f32[4,8,128,256]{3,2,1,0:T(8,128)}, /*index=5*/s32[]{:T(128)}) while((s32[]{:T(128)}, f32[8,128,256]{1,2,0:T(8,128)}, s32[]{:T(128)}, f32[4,8,256,256]{3,2,1,0:T(8,128)}, f32[4,8,128,256]{3,2,1,0:T(8,128)}, ...), condition=%wide.region_11.12_spmd, body=%wide.region_10.11_spmd.sunk | while | flops 805830656 | bytes 16777840 | solution.py:119
  649.1 6.1 fusion.106
  659.4 6.1 fusion.106
  669.7 6.1 fusion.106
  680.0 6.1 fusion.106
  686.1 4.0 convolution_add_fusion
  693.1 2.6 fusion.45
  (158 shorter events, 63.5 us)
Async XLA Ops:
  6.5 108.3 %all-gather.15.cloned.1.call-start = ((), (), s32[]{:S(2)}) async-start(), calls=%async_computation.1 | async-start | bytes 5242880 | tf_op jit(solution)/shard_map/all_gather | solution.py:9
  6.6 6.9 copy-start.23
  8.2 5.3 copy-start.26
  10.5 4.3 copy-start.29
  10.5 4.4 copy-start.25
  10.5 4.6 copy-start.19
  17.7 2.1 copy-start.21
  19.9 16.1 %copy-start.2 = (f32[256,8,128]{2,1,0:T(8,128)}, f32[256,8,128]{2,1,0:T(8,128)S(1)}, u32[]{:S(2)}) copy-start(f32[256,8,128]{2,1,0:T(8,128)S(1)} %get-tuple-element.269) | copy-start | bytes 3145732
  24.2 1.7 copy-start.6
  28.6 3.0 copy-start.30
  28.6 3.0 copy-start.24
  28.6 3.0 copy-start.27
  28.6 3.0 copy-start.28
  31.3 233.4 %all-gather.13.cloned.1.call-start = ((), (), s32[]{:S(2)}) async-start(), calls=%async_computation | async-start | bytes 10485760 | tf_op jit(solution)/shard_map/all_gather | solution.py:9
  34.5 2.9 copy-start.8
  34.5 2.9 copy-start.10
  35.9 1.5 copy-start.12
  40.2 361.0 %all-gather.21.cloned.1.call-start = ((), (), s32[]{:S(2)}) async-start(), calls=%async_computation.4 | async-start | bytes 5242880 | tf_op jit(solution)/shard_map/all_gather | solution.py:23
  319.3 2.9 copy-start.9
  319.3 2.9 copy-start.11
  322.0 228.8 %all-gather.17.cloned.1.call-start = ((), (), s32[]{:S(2)}) async-start(), calls=%async_computation.2 | async-start | bytes 10485760 | tf_op jit(solution)/shard_map/all_gather | solution.py:23
  328.2 256.7 %all-gather.23.cloned.1.call-start = ((), (), s32[]{:S(2)}) async-start(), calls=%async_computation.5 | async-start | bytes 5242880 | tf_op jit(solution)/shard_map/all_gather | solution.py:138
  404.8 239.9 %all-gather.19.cloned.1.call-start = ((), (), s32[]{:S(2)}) async-start(), calls=%async_computation.3 | async-start | bytes 10485760 | tf_op jit(solution)/shard_map/all_gather | solution.py:137
  556.3 2.1 copy-start.22
  561.1 4.9 copy-start.1
  647.5 1.5 copy-start
  657.8 1.5 copy-start
  668.1 1.5 copy-start
  678.4 1.5 copy-start
  686.1 4.0 copy-start.4
  690.1 2.5 copy-start.15
  691.4 1.7 copy-start.5
  (8 other events, 8.5 us)
Sparse Core Ops, SparseCore 0:
  31.4 83.4 all-gather.14
  116.4 148.1 all-gather.12
  322.1 78.9 all-gather.20
  402.6 148.1 all-gather.16
  552.2 32.6 all-gather.22
  586.3 58.2 all-gather.18
